TPU v7x, 256 devices: a whole 4x4x8 slice. The times are simulated.
256 devices in a mesh: expert: 64 (over z, y, core), tensor: 4 (over x).
Axes of the slice: x: 4, y: 4, z: 8, core: 2. Of those that a mesh axis runs over, the one named last changes fastest.
Arguments:
- tokens: bfloat16 [8192, 2048], P('expert', 'tensor'), may hold values from -6 to 6
- grad_out: bfloat16 [8192, 2048], P('expert', 'tensor'), may hold values from -1.1953125 to 1.1953125
- routes: int32 [8192, 2], P('expert'), may hold values from 0 to 15, all different within a row; in each aligned block of 128 rows (0 to 127, 128 to 255, ...) at most 20 rows name the same one
- gates: float32 [8192, 2], P('expert'), may hold values from 0.1 to 1
- w_up: bfloat16 [2048, 131072], P(None, ('expert', 'tensor')), may hold values from -0.125 to 0.125
- w_down: bfloat16 [131072, 2048], P(('expert', 'tensor')), may hold values from -0.0625 to 0.0625
Outputs:
- grad_tokens: bfloat16 [8192, 2048], P('expert', 'tensor')
- grad_up: float32 [2048, 131072], P(None, ('expert', 'tensor'))
- grad_down: float32 [131072, 2048], P(('expert', 'tensor'))
Inputs may be any that keep to these rules, and one draw needn't show every extreme that they name: `routes`: the two experts of a token differ. Among the tokens of one index of the expert axis no expert is named more than 20 times, and in every draw some expert is named exactly 20 times by the tokens of some index.
All inputs are finite; a program needn't handle non-finite values.
Results may differ from a plain program's by a relative error of at most 0.012.
Values may be sent and summed in bfloat16 or wider, within the bound.
A program may use at most 128 MiB of HBM per device.

v0:
```python
import jax
import jax.numpy as jnp
from jax import lax
from jax.sharding import PartitionSpec as P

EXP_FULL = 16
root_half = 0.7071067811865476
gauss_norm = 0.3989422804014327


def split_up(x, dim, size):
    shape = x.shape
    tiles = x.reshape(*shape[:dim], size, shape[dim] // size, *shape[dim + 1 :])
    return jnp.moveaxis(tiles, dim, 0)


def sum_at_owner(x, axis, dim):
    size = lax.axis_size(axis)
    tiles = lax.all_to_all(split_up(x, dim, size), axis, 0, 0, tiled=True)
    return jnp.sum(tiles.astype(jnp.float32), axis=0)


def gelu_value(v):
    return 0.5 * v * (1.0 + lax.erf(v * root_half))


def gelu_slope(v):
    return 0.5 * (1.0 + lax.erf(v * root_half)) + v * jnp.exp(-0.5 * v * v) * gauss_norm


def local(tokens, grad_out, routes, gates, w_up, w_down):
    expert_count = lax.axis_size("expert")
    experts = min(EXP_FULL, expert_count)
    group = expert_count // experts
    tok_dev = routes.shape[0]
    choose = routes.shape[1]
    capacity = group * (5 * tok_dev // (2 * expert_count))
    flat = routes.reshape(-1)
    onehot = (flat[:, None] == jnp.arange(experts, dtype=jnp.int32)[None, :]).astype(jnp.int32)
    rank = jnp.cumsum(onehot, axis=0, dtype=jnp.int32) - onehot
    dest = flat * capacity + jnp.sum(rank * onehot, axis=1)
    select = (jnp.arange(experts * capacity, dtype=jnp.int32)[:, None] == dest[None, :]).astype(
        jnp.bfloat16
    )
    full_tok, full_grad = (tokens, grad_out)
    width = full_tok.shape[1]
    repeated = jnp.repeat(full_tok, choose, axis=0)
    scaled = (full_grad[:, None, :].astype(jnp.float32) * gates[:, :, None]).astype(jnp.bfloat16)
    scaled = scaled.reshape(tok_dev * choose, width)
    packed = (
        jnp.stack(
            [
                jnp.dot(select, repeated, preferred_element_type=jnp.float32),
                jnp.dot(select, scaled, preferred_element_type=jnp.float32),
            ]
        )
        .astype(jnp.bfloat16)
        .reshape(2, experts, capacity, width)
    )
    outgoing = jnp.repeat(packed, group, axis=1)
    arrived = lax.all_to_all(outgoing, "expert", split_axis=1, concat_axis=1, tiled=True)
    arrived = lax.all_gather(arrived, "tensor", axis=3, tiled=True)
    rows = arrived.reshape(2, expert_count * capacity, arrived.shape[3])
    rows_x = rows[0]
    rows_y = rows[1]
    pre = jnp.dot(rows_x, w_up, preferred_element_type=jnp.float32)
    act = gelu_value(pre).astype(jnp.bfloat16)
    d_act = lax.dot_general(
        rows_y, w_down, (((1,), (1,)), ((), ())), preferred_element_type=jnp.float32
    )
    d_pre = (d_act * gelu_slope(pre)).astype(jnp.bfloat16)
    grad_up = lax.dot_general(
        rows_x, d_pre, (((0,), (0,)), ((), ())), preferred_element_type=jnp.float32
    )
    grad_down = lax.dot_general(
        act, rows_y, (((0,), (0,)), ((), ())), preferred_element_type=jnp.float32
    )
    partial_value = lax.dot_general(
        d_pre, w_up, (((1,), (1,)), ((), ())), preferred_element_type=jnp.float32
    )
    partial_value = lax.optimization_barrier(partial_value.astype(jnp.bfloat16)).astype(jnp.float32)
    summed = sum_at_owner(partial_value.astype(jnp.bfloat16), "tensor", 1)
    quarter = summed.shape[1]
    back = summed.reshape(expert_count, capacity, quarter)
    returned = lax.all_to_all(
        back.astype(jnp.bfloat16), "expert", split_axis=0, concat_axis=0, tiled=True
    ).astype(back.dtype)
    combined = returned.reshape(experts, group, capacity, quarter).sum(axis=1)
    combined = combined.reshape(experts * capacity, quarter)
    grad_tokens = combined[dest].reshape(tok_dev, choose, quarter).sum(axis=1).astype(jnp.bfloat16)
    return (grad_tokens, grad_up, grad_down)


def solution(mesh):
    return jax.shard_map(
        local,
        mesh=mesh,
        in_specs=(
            P("expert", "tensor"),
            P("expert", "tensor"),
            P("expert", None),
            P("expert", None),
            P(None, ("expert", "tensor")),
            P(("expert", "tensor"), None),
        ),
        out_specs=(
            P("expert", "tensor"),
            P(None, ("expert", "tensor")),
            P(("expert", "tensor"), None),
        ),
        check_vma=False,
    )
```

profile of v0, /device:TPU:1, one launch (start us, length us, event | category | flops | bytes accessed | tf_op | source)
XLA Modules:
  0.0 406.1 jit_solution(18192644028344596392)
XLA Ops:
  7.2 0.9 copy.14
  8.3 0.1 reshape.145
  8.5 0.6 reduce-window.6
  9.0 0.2 slice_reduce_fusion.2
  9.4 1.0 mul.84
  10.4 0.4 mul.85
  10.8 0.8 copy.17
  11.7 1.0 broadcast_in_dim.4
  12.9 0.3 fusion.7
  13.2 0.3 fusion.8
  13.6 0.7 copy.18
  14.3 1.6 broadcast_in_dim.5
  15.9 75.8 %all_to_all.15 = bf16[2,64,20,512]{3,0,2,1:T(2,128)(2,1)} all-to-all(bf16[2,64,20,512]{3,0,2,1:T(2,128)(2,1)S(1)} %bitcast.52), channel_id=1, replica_groups=mesh['expert'=64,'tensor'=4] {'expert'}, dimensions={1} | all-to-all | bytes 5242880 | tf_op jit(solution)/shard_map/all_to_all | solution.py:61
  91.7 101.8 %all-gather.2.cloned.1.call-done = bf16[2,64,20,2048]{3,0,2,1:T(2,128)(2,1)} async-done(((bf16[2,64,20,512]{3,0,2,1:T(2,128)(2,1)}), bf16[2,64,20,2048]{3,0,2,1:T(2,128)(2,1)}) %all-gather.2.cloned.1.call-update) | async-done | bytes 10485776 | tf_op jit(solution)/shard_map/all_gather | solution.py:62
  193.5 52.4 %slice_reduce_fusion = (bf16[64,20,2048]{2,1,0:T(8,128)(2,1)}, bf16[64,20,2048]{2,1,0:T(8,128)(2,1)}) fusion(bf16[2,64,20,2048]{3,0,2,1:T(2,128)(2,1)} %all-gather.2.cloned.1.call-done), kind=kLoop, calls=%fused_computation.1 | loop fusion | bytes 20971520 | tf_op jit(solution)/shard_map/slice | solution.py:64
  245.9 9.0 %squeeze.7 = bf16[1280,2048]{1,0:T(8,128)(2,1)} reshape(bf16[64,20,2048]{2,1,0:T(8,128)(2,1)} %get-tuple-element.3) | data formatting | bytes 10485760 | tf_op jit(solution)/shard_map/squeeze | solution.py:64
  254.9 9.0 %squeeze.6 = bf16[1280,2048]{1,0:T(8,128)(2,1)} reshape(bf16[64,20,2048]{2,1,0:T(8,128)(2,1)} %get-tuple-element.4) | data formatting | bytes 10485760 | tf_op jit(solution)/shard_map/squeeze | solution.py:65
  263.9 4.9 %fusion.23 = f32[1280,512]{1,0:T(8,128)S(1)} fusion(bf16[1280,2048]{1,0:T(8,128)(2,1)} %squeeze.7, bf16[2048,512]{1,0:T(8,128)(2,1)S(1)} %copy-done), kind=kOutput, calls=%fused_computation.46 | convolution fusion | flops 2684354560 | bytes 9961472 | tf_op jit(solution)/shard_map/dot_general | solution.py:66
  268.9 3.9 fusion
  272.8 3.2 convolution_convert_fusion
  276.0 0.5 copy.27
  276.5 61.2 %all_to_all.16 = bf16[4,1280,512]{2,1,0:T(8,128)(2,1)} all-to-all(bf16[4,1280,512]{2,1,0:T(8,128)(2,1)S(1)} %bitcast.51), channel_id=1, replica_groups=mesh['expert'=64,'tensor'=4] {'tensor'}, dimensions={0} | all-to-all | bytes 10485760 | tf_op jit(solution)/shard_map/all_to_all | solution.py:19
  337.7 4.2 %reduce_sum.42 = bf16[1280,512]{1,0:T(8,128)(2,1)S(1)} reduce(bf16[4,1280,512]{2,1,0:T(8,128)(2,1)} %all_to_all.16, bf16[]{:T(256)} %constant.24.clone.1), dimensions={0}, to_apply=%region_3.4 | reduce | flops 1966080 | bytes 6553602 | tf_op jit(solution)/shard_map/reduce_sum | solution.py:20
  341.9 1.3 convert_element_type.46
  343.2 14.1 %all-to-all-start.2 = ((bf16[64,20,512]{2,1,0:T(8,128)(2,1)}), bf16[64,20,512]{2,1,0:T(8,128)(2,1)S(1)}, u32[]{:S(2)}, u32[]{:S(2)}) async-start(bf16[64,20,512]{2,1,0:T(8,128)(2,1)} %convert_element_type.46), calls=%async_computation.2 | async-start | bytes 3145728 | tf_op jit(solution)/shard_map/all_to_all | solution.py:85
  357.6 8.0 %fusion.24 = f32[2048,512]{1,0:T(8,128)} fusion(bf16[1280,2048]{1,0:T(8,128)(2,1)} %squeeze.7, bf16[1280,512]{1,0:T(8,128)(2,1)} %copy-done.7), kind=kOutput, calls=%fused_computation.47 | convolution fusion | flops 2684354560 | bytes 10747904 | tf_op jit(solution)/shard_map/dot_general | solution.py:72
  365.6 4.5 %fusion.5 = f32[512,2048]{1,0:T(8,128)} fusion(bf16[1280,2048]{1,0:T(8,128)(2,1)S(1)} %bitcast.50, f32[1280,512]{1,0:T(8,128)S(1)} %copy-done.4), kind=kOutput, calls=%fused_computation.15 | convolution fusion | flops 2687631360 | bytes 12058624 | tf_op jit(solution)/shard_map/dot_general | solution.py:75
  370.1 26.2 %all-to-all-done.2 = bf16[64,20,512]{2,1,0:T(8,128)(2,1)S(1)} async-done(((bf16[64,20,512]{2,1,0:T(8,128)(2,1)}), bf16[64,20,512]{2,1,0:T(8,128)(2,1)S(1)}, u32[]{:S(2)}, u32[]{:S(2)}) %all-to-all-start.2) | async-done | bytes 1310752 | tf_op jit(solution)/shard_map/all_to_all | solution.py:85
  396.3 0.3 convert_reduce_fusion
  396.7 1.0 gather_fusion
  397.6 0.3 reshape.153
  397.9 1.3 reduce_sum.45
  (39 shorter events, 1.1 us)
Async XLA Ops:
  7.2 256.7 %copy-start = (bf16[2048,512]{1,0:T(8,128)(2,1)S(1)}, bf16[2048,512]{1,0:T(8,128)(2,1)}, u32[]{:S(2)}) copy-start(bf16[2048,512]{1,0:T(8,128)(2,1)} %param.10) | copy-start | bytes 6291460
  7.2 186.3 %all-gather.2.cloned.1.call-start = ((), (), s32[]{:S(2)}) async-start(), calls=%async_computation.3 | async-start | bytes 13107200 | tf_op jit(solution)/shard_map/all_gather | solution.py:62
  263.9 5.0 %copy-start.2 = (bf16[1280,2048]{1,0:T(8,128)(2,1)S(1)}, bf16[1280,2048]{1,0:T(8,128)(2,1)}, u32[]{:S(2)}) copy-start(bf16[1280,2048]{1,0:T(8,128)(2,1)} %squeeze.6) | copy-start | bytes 15728644
  263.9 5.0 %copy-start.6 = (bf16[512,2048]{1,0:T(8,128)(2,1)S(1)}, bf16[512,2048]{1,0:T(8,128)(2,1)}, u32[]{:S(2)}) copy-start(bf16[512,2048]{1,0:T(8,128)(2,1)} %param.11) | copy-start | bytes 6291460
  268.9 3.9 copy-start.3
  272.7 3.2 copy-start.7
  341.8 15.4 %copy-start.5 = (s32[128,2]{0,1:T(2,128)S(1)}, s32[128,2]{0,1:T(2,128)}, u32[]{:S(2)}) copy-start(s32[128,2]{0,1:T(2,128)} %param.8) | copy-start | bytes 3076
  343.2 22.4 %slice-start = ((s8[5242880]{0:T(1024)(128)(4,1)}), s8[1048576]{0:T(1024)(128)(4,1)S(1)}, s32[]{:S(2)}) async-start(s8[5242880]{0:T(1024)(128)(4,1)} %bitcast.49), calls=%async_computation.4 | async-start | bytes 2097152
  343.2 53.2 %all-to-all-start.2 = ((bf16[64,20,512]{2,1,0:T(8,128)(2,1)}), bf16[64,20,512]{2,1,0:T(8,128)(2,1)S(1)}, u32[]{:S(2)}, u32[]{:S(2)}) async-start(bf16[64,20,512]{2,1,0:T(8,128)(2,1)} %convert_element_type.46), calls=%async_computation.2 | async-start | bytes 3145728 | tf_op jit(solution)/shard_map/all_to_all | solution.py:85
  357.6 8.0 %slice-start.1 = ((s8[5242880]{0:T(1024)(128)(4,1)}), s8[4194304]{0:T(1024)(128)(4,1)S(1)}, s32[]{:S(2)}) async-start(s8[5242880]{0:T(1024)(128)(4,1)} %bitcast.49), calls=%async_computation.5 | async-start | bytes 8388608
  357.6 8.0 %copy-start.4 = (f32[1280,512]{1,0:T(8,128)S(1)}, f32[1280,512]{1,0:T(8,128)}, u32[]{:S(2)}) copy-start(f32[1280,512]{1,0:T(8,128)} %copy-done.3) | copy-start | bytes 7864324
  396.6 2.7 copy-start.1
Sparse Core Ops, SparseCore 0:
  91.9 101.5 all-gather.1
where the time goes:
time: 407 us; the launch traced here: 406 us
  blocking collectives  137 us (34%)
  waiting for transfers between devices  128 us (31%)
  local copies, waits for them, and re-layouts  81 us (20%)
  matrix products  25.2 us (6%)
  between operations  14.3 us (4%)
  starting transfers between devices  14.1 us (3%)
  other arithmetic  6.57 us (2%)
    all_gather x1, waiting for transfers between devices, local(): arrived = lax.all_gather(arrived, 'tensor', axis=3, tiled=True)  102 us
    all_to_all x1, blocking collectives, local(): lax.all_to_all(outgoing, 'expert', split_axis=1, concat_axis=1, tiled=True)  75.8 us
    all_to_all x1, blocking collectives, sum_at_owner(): tiles = lax.all_to_all(split_up(x, dim, size), axis, 0, 0, tiled=True)  61.2 us
    slice x1, local copies, waits for them, and re-layouts, local(): rows_x = rows[0]  52.4 us
    all_to_all x1, waiting for transfers between devices, local(): lax.all_to_all(back.astype(jnp.bfloat16), 'expert', split_axis=0, concat_...  26.2 us
    all_to_all x1, starting transfers between devices, local(): lax.all_to_all(back.astype(jnp.bfloat16), 'expert', split_axis=0, concat_...  14.1 us
    squeeze x1, local copies, waits for them, and re-layouts, local(): rows_y = rows[1]  9 us
    squeeze x1, local copies, waits for them, and re-layouts, local(): rows_x = rows[0]  8.99 us
  transfers between devices with their start and end apart: 2, of which 2 were waited for; matrix products, arithmetic and copies ran while one was open for 3% of the time, Pallas kernels for 0%

commit v1 on v0

--- a/solution.py
+++ b/solution.py
@@ -1,11 +1,22 @@
+import functools
 import jax
 import jax.numpy as jnp
 from jax import lax
 from jax.sharding import PartitionSpec as P
+from jax.lax import all_to_all, axis_size
 
 EXP_FULL = 16
 root_half = 0.7071067811865476
 gauss_norm = 0.3989422804014327
+
+
+def resolve_lines_on_mesh(z_in, which_axis):
+    return jnp.concatenate(
+        all_to_all(jnp.stack([z_in] * axis_size(which_axis), axis=0), which_axis, 0, 0), axis=3
+    )
+
+
+pass_vector_up = functools.partial(resolve_lines_on_mesh, which_axis="tensor")
 
 
 def split_up(x, dim, size):
@@ -59,7 +70,7 @@
     )
     outgoing = jnp.repeat(packed, group, axis=1)
     arrived = lax.all_to_all(outgoing, "expert", split_axis=1, concat_axis=1, tiled=True)
-    arrived = lax.all_gather(arrived, "tensor", axis=3, tiled=True)
+    arrived = pass_vector_up(arrived)
     rows = arrived.reshape(2, expert_count * capacity, arrived.shape[3])
     rows_x = rows[0]
     rows_y = rows[1]

time: 407 us -> 378 us (0.929)
  blocking collectives: 137 us -> 263 us
  waiting for transfers between devices: 128 us -> 26.2 us
  local copies, waits for them, and re-layouts: 81 us -> 48.9 us
  between operations: 14.3 us -> 0.95 us
  starting transfers between devices: 14.1 us -> 7.05 us
    all_to_all x0 -> x1, blocking collectives: none -> 124 us  [resolve_lines_on_mesh(): all_to_all(jnp.stack([z_in] * axis_size(which_axis), axis=0), which_axis,...]
    all_gather x1 -> x0, waiting for transfers between devices: 102 us -> none  [local(): arrived = lax.all_gather(arrived, 'tensor', axis=3, tiled=True)]
    slice x1 -> x2, local copies, waits for them, and re-layouts: 52.4 us -> 16.3 us  [local(): rows_x = rows[0]]
    squeeze x2 -> x0, local copies, waits for them, and re-layouts: 18 us -> none  [the longest x1 9 us: local(): rows_y = rows[1]]
    unnamed x22 -> x28, local copies, waits for them, and re-layouts: 1.77 us -> 10.3 us
    all_to_all x1, starting transfers between devices: 14.1 us -> 7.05 us  [local(): lax.all_to_all(back.astype(jnp.bfloat16), 'expert', split_axis=0, concat_...]
    another operation x1 -> x2, local copies, waits for them, and re-layouts: 0.01 us -> 6.91 us  [the longest x1 6.91 us: resolve_lines_on_mesh(): jnp.stack([z_in] * axis_size(which_axis), axis=0)]
  transfers between devices with their start and end apart: 2 -> 1, of which waited for: 2 -> 1; matrix products, arithmetic and copies ran while one was open for 3% -> 3% of each run, Pallas kernels for 0% -> 0%
where the time goes in v1:
time: 378 us; the launch traced here: 377 us
  blocking collectives  263 us (70%)
  local copies, waits for them, and re-layouts  48.9 us (13%)
  waiting for transfers between devices  26.2 us (7%)
  matrix products  23.2 us (6%)
  other arithmetic  8.06 us (2%)
  starting transfers between devices  7.05 us (2%)
    all_to_all x1, blocking collectives, resolve_lines_on_mesh(): all_to_all(jnp.stack([z_in] * axis_size(which_axis), axis=0), which_axis,...  124 us
    all_to_all x1, blocking collectives, local(): lax.all_to_all(outgoing, 'expert', split_axis=1, concat_axis=1, tiled=True)  75.7 us
    all_to_all x1, blocking collectives, sum_at_owner(): tiles = lax.all_to_all(split_up(x, dim, size), axis, 0, 0, tiled=True)  62.5 us
    all_to_all x1, waiting for transfers between devices, local(): lax.all_to_all(back.astype(jnp.bfloat16), 'expert', split_axis=0, concat_...  26.2 us
    slice x2, local copies, waits for them, and re-layouts, local(): rows_x = rows[0]  16.3 us
    unnamed x28, local copies, waits for them, and re-layouts  10.3 us
    dot_general x1, matrix products, local(): lax.dot_general(rows_x, d_pre, (((0,), (0,)), ((), ())), preferred_elemen...  7.96 us
  transfers between devices with their start and end apart: 1, of which 1 were waited for; matrix products, arithmetic and copies ran while one was open for 3% of the time, Pallas kernels for 0%

profile of v1, /device:TPU:1, one launch (start us, length us, event | category | flops | bytes accessed | tf_op | source)
XLA Modules:
  0.0 377.0 jit_solution(13304551178562915950)
XLA Ops:
  0.7 0.9 copy.24
  1.9 0.6 reduce-window.6
  2.8 0.8 copy.27
  3.7 1.0 broadcast_in_dim.4
  4.9 1.0 mul.84
  5.9 0.4 mul.85
  7.1 0.7 copy.28
  7.8 1.6 broadcast_in_dim.5
  9.4 75.7 %all_to_all.20 = bf16[2,64,20,512]{3,0,2,1:T(2,128)(2,1)S(1)} all-to-all(bf16[2,64,20,512]{3,0,2,1:T(2,128)(2,1)S(1)} %bitcast.66), channel_id=1, replica_groups=mesh['expert'=64,'tensor'=4] {'expert'}, dimensions={1} | all-to-all | bytes 5242880 | tf_op jit(solution)/shard_map/all_to_all | solution.py:72
  85.0 2.4 copy.29
  87.4 6.9 %stack.5 = bf16[4,2,64,20,512]{4,2,3,1,0:T(8,128)(2,1)} broadcast(bf16[2,64,20,512]{3,1,2,0:T(8,128)(2,1)} %copy.29), dimensions={1,2,3,4} | broadcast | bytes 13107200 | tf_op jit(solution)/shard_map/stack | solution.py:15
  94.3 124.5 %all_to_all.21 = bf16[4,2,64,20,512]{4,2,3,1,0:T(8,128)(2,1)} all-to-all(bf16[4,2,64,20,512]{4,2,3,1,0:T(8,128)(2,1)} %stack.5), channel_id=1, replica_groups=mesh['expert'=64,'tensor'=4] {'tensor'}, dimensions={0} | all-to-all | bytes 20971520 | tf_op jit(solution)/shard_map/all_to_all | solution.py:15
  218.8 9.6 %fusion.23 = (bf16[1,64,20,4,512]{4,1,2,0,3:T(8,128)(2,1)}, bf16[1,64,20,4,512]{4,1,2,0,3:T(8,128)(2,1)}) fusion(bf16[2,64,20,4,512]{4,1,2,0,3:T(8,128)(2,1)} %bitcast.56), kind=kLoop, calls=%fused_computation.44 | loop fusion | bytes 20971520 | tf_op jit(solution)/shard_map/slice | solution.py:75
  228.5 6.7 %copy.31 = bf16[1,64,20,4,512]{4,3,2,1,0:T(4,128)(2,1)S(1)} copy(bf16[1,64,20,4,512]{4,1,2,0,3:T(8,128)(2,1)} %get-tuple-element.3) | data formatting | bytes 10485760 | tf_op jit(solution)/shard_map/slice | solution.py:75
  235.2 4.6 %copy.37 = bf16[160,8,4,512]{3,1,2,0:T(8,128)(2,1)} copy(bf16[160,8,4,512]{3,2,1,0:T(4,128)(2,1)S(1)} %bitcast.63) | data formatting | bytes 10485760
  239.7 4.0 %copy.30 = bf16[1,64,20,4,512]{4,3,2,1,0:T(4,128)(2,1)S(1)} copy(bf16[1,64,20,4,512]{4,1,2,0,3:T(8,128)(2,1)S(1)} %bitcast.62) | data formatting | bytes 10485760 | tf_op jit(solution)/shard_map/slice | solution.py:76
  243.8 2.5 copy.36
  246.3 2.9 fusion.24
  249.3 1.5 copy-done.2
  250.8 3.9 %fusion = bf16[1280,512]{1,0:T(8,128)(2,1)S(1)} fusion(bf16[1280,2048]{1,0:T(8,128)(2,1)S(1)} %bitcast.57, bf16[512,2048]{1,0:T(8,128)(2,1)S(1)} %copy-done.6, f32[1280,512]{1,0:T(8,128)S(1)} %fusion.24), kind=kOutput, calls=%fused_computation.6 | convolution fusion | flops 2690908160 | bytes 11272192 | tf_op jit(solution)/shard_map/dot_general | solution.py:79
  254.7 3.2 convolution_convert_fusion
  257.9 0.5 copy.40
  258.4 62.5 %all_to_all.22 = bf16[4,1280,512]{2,1,0:T(8,128)(2,1)} all-to-all(bf16[4,1280,512]{2,1,0:T(8,128)(2,1)S(1)} %bitcast.65), channel_id=1, replica_groups=mesh['expert'=64,'tensor'=4] {'tensor'}, dimensions={0} | all-to-all | bytes 10485760 | tf_op jit(solution)/shard_map/all_to_all | solution.py:30
  320.9 4.2 %reduce_sum.42 = bf16[1280,512]{1,0:T(8,128)(2,1)S(1)} reduce(bf16[4,1280,512]{2,1,0:T(8,128)(2,1)} %all_to_all.22, bf16[]{:T(256)} %constant.24.clone.1), dimensions={0}, to_apply=%region_3.4 | reduce | flops 1966080 | bytes 6553602 | tf_op jit(solution)/shard_map/reduce_sum | solution.py:31
  325.1 1.4 convert_element_type.46
  326.5 7.1 %all-to-all-start.3 = ((bf16[64,20,512]{2,1,0:T(8,128)(2,1)}), bf16[64,20,512]{2,1,0:T(8,128)(2,1)}, u32[]{:S(2)}, u32[]{:S(2)}) async-start(bf16[64,20,512]{2,1,0:T(8,128)(2,1)} %convert_element_type.46), calls=%async_computation.3 | async-start | bytes 3145728 | tf_op jit(solution)/shard_map/all_to_all | solution.py:96
  333.8 8.0 %fusion.25 = f32[2048,512]{1,0:T(8,128)} fusion(bf16[1280,2048]{1,0:T(8,128)(2,1)} %bitcast.67, bf16[1280,512]{1,0:T(8,128)(2,1)} %copy-done.7), kind=kOutput, calls=%fused_computation.46 | convolution fusion | flops 2684354560 | bytes 10747904 | tf_op jit(solution)/shard_map/dot_general | solution.py:83
  341.8 4.5 %fusion.5 = f32[512,2048]{1,0:T(8,128)} fusion(bf16[1280,2048]{1,0:T(8,128)(2,1)S(1)} %bitcast.60, f32[1280,512]{1,0:T(8,128)S(1)} %copy-done.3), kind=kOutput, calls=%fused_computation.13 | convolution fusion | flops 2687631360 | bytes 12058624 | tf_op jit(solution)/shard_map/dot_general | solution.py:86
  346.4 26.2 %all-to-all-done.3 = bf16[64,20,512]{2,1,0:T(8,128)(2,1)} async-done(((bf16[64,20,512]{2,1,0:T(8,128)(2,1)}), bf16[64,20,512]{2,1,0:T(8,128)(2,1)}, u32[]{:S(2)}, u32[]{:S(2)}) %all-to-all-start.3) | async-done | bytes 1310752 | tf_op jit(solution)/shard_map/all_to_all | solution.py:96
  372.6 1.7 convert_reduce_fusion
  374.4 1.0 gather_fusion
  375.7 1.3 reduce_sum.45
  (46 shorter events, 2.3 us)
Async XLA Ops:
  0.6 245.7 %copy-start = (bf16[2048,512]{1,0:T(8,128)(2,1)S(1)}, bf16[2048,512]{1,0:T(8,128)(2,1)}, u32[]{:S(2)}) copy-start(bf16[2048,512]{1,0:T(8,128)(2,1)} %param.10) | copy-start | bytes 6291460
  228.5 11.3 %slice-start.2 = ((s8[5242880]{0:T(1024)(128)(4,1)}), s8[4194304]{0:T(1024)(128)(4,1)S(1)}, s32[]{:S(2)}) async-start(s8[5242880]{0:T(1024)(128)(4,1)} %bitcast.61), calls=%async_computation.6 | async-start | bytes 8388608
  235.1 4.6 %slice-start.3 = ((s8[5242880]{0:T(1024)(128)(4,1)}), s8[1048576]{0:T(1024)(128)(4,1)S(1)}, s32[]{:S(2)}) async-start(s8[5242880]{0:T(1024)(128)(4,1)} %bitcast.61), calls=%async_computation.7 | async-start | bytes 2097152
  243.8 2.6 copy-start.4
  246.3 3.0 copy-start.1
  246.3 4.4 %copy-start.6 = (bf16[512,2048]{1,0:T(8,128)(2,1)S(1)}, bf16[512,2048]{1,0:T(8,128)(2,1)}, u32[]{:S(2)}) copy-start(bf16[512,2048]{1,0:T(8,128)(2,1)} %param.11) | copy-start | bytes 6291460
  249.3 1.5 copy-start.2
  254.7 3.2 copy-start.7
  325.1 8.5 %copy-start.5 = (s32[128,2]{0,1:T(2,128)S(1)}, s32[128,2]{0,1:T(2,128)}, u32[]{:S(2)}) copy-start(s32[128,2]{0,1:T(2,128)} %param.8) | copy-start | bytes 3076
  326.4 15.4 %slice-start = ((s8[5242880]{0:T(1024)(128)(4,1)}), s8[1048576]{0:T(1024)(128)(4,1)S(1)}, s32[]{:S(2)}) async-start(s8[5242880]{0:T(1024)(128)(4,1)} %bitcast.58), calls=%async_computation.4 | async-start | bytes 2097152
  326.5 46.1 %all-to-all-start.3 = ((bf16[64,20,512]{2,1,0:T(8,128)(2,1)}), bf16[64,20,512]{2,1,0:T(8,128)(2,1)}, u32[]{:S(2)}, u32[]{:S(2)}) async-start(bf16[64,20,512]{2,1,0:T(8,128)(2,1)} %convert_element_type.46), calls=%async_computation.3 | async-start | bytes 3145728 | tf_op jit(solution)/shard_map/all_to_all | solution.py:96
  333.8 8.0 %slice-start.1 = ((s8[5242880]{0:T(1024)(128)(4,1)}), s8[4194304]{0:T(1024)(128)(4,1)S(1)}, s32[]{:S(2)}) async-start(s8[5242880]{0:T(1024)(128)(4,1)} %bitcast.58), calls=%async_computation.5 | async-start | bytes 8388608
  333.8 8.0 %copy-start.3 = (f32[1280,512]{1,0:T(8,128)S(1)}, f32[1280,512]{1,0:T(8,128)}, u32[]{:S(2)}) copy-start(f32[1280,512]{1,0:T(8,128)} %copy-done.2) | copy-start | bytes 7864324
